TPU v7x, 256 devices: a whole 4x4x8 slice. The times are simulated.
256 devices in a mesh: dp: 8 (over z_hi, x), expert: 32 (over z_lo, y, core).
Axes of the slice: x: 4, y: 4, z: 8 (z_hi: 2, z_lo: 4; z = z_hi * 4 + z_lo), core: 2. Of those that a mesh axis runs over, the one named last changes fastest.
Arguments:
- tokens: bfloat16 [8192, 7168], P('expert', 'dp'), may hold values from -6 to 6
- cotangent: bfloat16 [8192, 7168], P('expert', 'dp'), may hold values from -6 to 6
- routing: int32 [8192, 8], P('expert'), may hold values from 0 to 255, as said below
- gate_values: float32 [8192, 8], P('expert'), may hold values from 0.05 to 0.6
- hidden_weight: bfloat16 [32, 7168, 2048], P('expert', 'dp'), may hold values from -0.0625 to 0.0625
- output_weight: bfloat16 [32, 1024, 7168], P('expert', None, 'dp'), may hold values from -0.1875 to 0.1875
Outputs:
- mixed: bfloat16 [8192, 7168], P('expert', 'dp')
- token_grad: bfloat16 [8192, 7168], P('expert', 'dp')
- hidden_grad: bfloat16 [32, 7168, 2048], P('expert', 'dp')
- output_grad: bfloat16 [32, 1024, 7168], P('expert', None, 'dp')
Inputs may be any that keep to these rules, and one draw needn't show every extreme that they name: `routing`: each row names 8 different experts. Within the 256 rows of one index of expert no expert is named by more than 16 rows, and in every such block some experts below 32 are named by exactly 16 rows.
All inputs are finite; a program needn't handle non-finite values.
Results may differ from a plain program's by a relative error of at most 0.022.
Values may be sent and summed in bfloat16 or wider, within the bound.
A program may use at most 64 MiB of HBM per device.

v0:
```python
import jax
import jax.numpy as jnp
from jax import lax
from jax.sharding import PartitionSpec as P

ROUTED = 256


def slot_table(routing_block, gate_block, expert_count, slot_count):
    tok_count = routing_block.shape[0]
    picked = routing_block.reshape(-1)
    onehot = (picked[:, None] == jnp.arange(expert_count, dtype=jnp.int32)[None, :]).astype(
        jnp.int32
    )
    earlier = jnp.cumsum(onehot, axis=0) - onehot
    ranking = jnp.sum(earlier * onehot, axis=1)
    slot_index = (picked * slot_count + ranking).reshape(tok_count, -1)
    target = jnp.arange(expert_count * slot_count, dtype=jnp.int32)
    matched = slot_index[None, :, :] == target[:, None, None]
    placed = jnp.any(matched, axis=2).astype(jnp.float32)
    gate_slot = jnp.sum(
        jnp.where(matched, gate_block[None, :, :], jnp.zeros_like(gate_block)[None, :, :]),
        axis=(1, 2),
    )
    return (placed, gate_slot)


def activate(hidden, half_width):
    gate_part = hidden[:, :half_width]
    up_part = hidden[:, half_width:]
    return (gate_part * jax.nn.sigmoid(gate_part) * up_part).astype(jnp.bfloat16)


def activate_grad(hidden, act_grad, half_width):
    gate_part = hidden[:, :half_width]
    up_part = hidden[:, half_width:]
    sigmoid_gate = jax.nn.sigmoid(gate_part)
    gate_grad = act_grad * up_part * sigmoid_gate * (1.0 + gate_part * (1.0 - sigmoid_gate))
    up_grad = act_grad * gate_part * sigmoid_gate
    return jnp.concatenate([gate_grad, up_grad], axis=1).astype(jnp.bfloat16)


def body(tokens, cotangent, routing, gate_values, hidden_weight, output_weight):
    tok_count, column_width = tokens.shape
    pick_count = routing.shape[1]
    expert_count = lax.axis_size("expert")
    slot_count = 2 * tok_count * pick_count // ROUTED
    row_total = expert_count * slot_count
    contract_cols = (((1,), (1,)), ((), ()))
    contract_rows = (((0,), (0,)), ((), ()))
    placed, gate_slot = slot_table(routing, gate_values, expert_count, slot_count)
    placed_half = placed.astype(jnp.bfloat16)
    send_shape = (expert_count, slot_count, column_width)
    token_rows = (
        jnp.dot(placed_half, tokens, preferred_element_type=jnp.float32)
        .astype(jnp.bfloat16)
        .reshape(send_shape)
    )
    cot_rows = (
        (gate_slot[:, None] * jnp.dot(placed_half, cotangent, preferred_element_type=jnp.float32))
        .astype(jnp.bfloat16)
        .reshape(send_shape)
    )
    inner_weight = hidden_weight[0]
    outer_weight = output_weight[0]
    half_width = outer_weight.shape[0]
    arrived = (
        lax.all_to_all(token_rows, "expert", split_axis=0, concat_axis=0, tiled=True),
        lax.all_to_all(cot_rows, "expert", split_axis=0, concat_axis=0, tiled=True),
    )
    expert_rows = arrived[0].reshape(row_total, column_width)
    scaled_cot = arrived[1].reshape(row_total, column_width)
    partial_hidden = jnp.dot(expert_rows, inner_weight, preferred_element_type=jnp.float32)
    hidden = lax.psum(partial_hidden.astype(jnp.bfloat16), "dp").astype(jnp.float32)
    active = activate(hidden, half_width)
    expert_out = jnp.dot(active, outer_weight, preferred_element_type=jnp.float32).astype(
        jnp.bfloat16
    )
    partial_act = lax.dot_general(
        scaled_cot, outer_weight, contract_cols, preferred_element_type=jnp.float32
    )
    act_grad = lax.psum(partial_act.astype(jnp.bfloat16), "dp").astype(jnp.float32)
    hidden_cot = activate_grad(hidden, act_grad, half_width)
    output_grad = lax.dot_general(
        active, scaled_cot, contract_rows, preferred_element_type=jnp.float32
    ).astype(jnp.bfloat16)
    hidden_grad = lax.dot_general(
        expert_rows, hidden_cot, contract_rows, preferred_element_type=jnp.float32
    ).astype(jnp.bfloat16)
    row_grad = lax.dot_general(
        hidden_cot, inner_weight, contract_cols, preferred_element_type=jnp.float32
    ).astype(jnp.bfloat16)
    returned = (
        lax.all_to_all(
            expert_out.reshape(send_shape), "expert", split_axis=0, concat_axis=0, tiled=True
        ),
        lax.all_to_all(
            row_grad.reshape(send_shape), "expert", split_axis=0, concat_axis=0, tiled=True
        ),
    )
    back_out = returned[0]
    back_grad = returned[1]
    back_out = back_out.reshape(row_total, column_width)
    back_grad = back_grad.reshape(row_total, column_width)
    weighted = placed * gate_slot[:, None]
    mixed = lax.dot_general(
        weighted,
        back_out.astype(jnp.float32),
        contract_rows,
        precision=lax.Precision.HIGHEST,
        preferred_element_type=jnp.float32,
    ).astype(jnp.bfloat16)
    token_grad = lax.dot_general(
        placed_half, back_grad, contract_rows, preferred_element_type=jnp.float32
    ).astype(jnp.bfloat16)
    return (mixed, token_grad, hidden_grad[None], output_grad[None])


def solution(mesh):
    return jax.shard_map(
        body,
        mesh=mesh,
        in_specs=(
            P("expert", "dp"),
            P("expert", "dp"),
            P("expert", None),
            P("expert", None),
            P("expert", "dp", None),
            P("expert", None, "dp"),
        ),
        out_specs=(
            P("expert", "dp"),
            P("expert", "dp"),
            P("expert", "dp", None),
            P("expert", None, "dp"),
        ),
        check_vma=False,
    )
```

profile of v0, /device:TPU:1, one launch (start us, length us, event | category | flops | bytes accessed | tf_op | source)
XLA Modules:
  0.0 334.4 jit_solution(6971142851061227383)
XLA Ops:
  7.2 0.0 copy-start
  7.2 0.0 copy-start.6
  7.2 0.0 copy-start.7
  7.2 0.0 copy-start.9
  7.2 1.0 copy.26
  8.2 0.1 eq.42
  8.3 0.1 eq.38
  8.4 9.1 %reduce-window.6 = s32[32,16,128]{2,1,0:T(8,128)S(1)} reduce-window(s32[32,16,128]{2,1,0:T(8,128)S(1)} %fusion.32, s32[]{:T(128)} %constant.6.clone.1), window={size=1x1x128 pad=0_0x0_0x127_0}, to_apply=%region_0.0 | reduce-window | flops 8323072 | bytes 524292 | tf_op jit(solution)/shard_map/reduce-window
  17.5 0.1 slice.18
  17.7 0.2 copy.31
  17.9 0.2 reduce-window.9
  18.1 0.1 broadcast_add_fusion
  18.2 0.0 copy-start.5
  18.2 0.1 fusion.29
  18.4 0.1 reduce_sum.21
  18.5 0.1 copy.30
  18.5 0.0 copy-done.6
  18.5 1.9 fusion
  20.5 0.0 copy-done.7
  20.5 1.3 select_reduce_fusion
  21.7 0.0 copy-done.9
  21.7 1.4 multiply_convert_fusion.1
  23.1 10.2 %all-to-all-start.2 = ((bf16[32,16,896]{2,1,0:T(8,128)(2,1)}), bf16[32,16,896]{2,1,0:T(8,128)(2,1)S(1)}, u32[]{:S(2)}, u32[]{:S(2)}) async-start(bf16[32,16,896]{2,1,0:T(8,128)(2,1)} %bitcast.65), calls=%async_computation.2 | async-start | bytes 1835008 | tf_op jit(solution)/shard_map/all_to_all | solution.py:69
  33.3 0.0 copy-done.5
  33.3 1.4 convolution_convert_fusion
  34.7 22.7 %all-to-all-done.2 = bf16[32,16,896]{2,1,0:T(8,128)(2,1)S(1)} async-done(((bf16[32,16,896]{2,1,0:T(8,128)(2,1)}), bf16[32,16,896]{2,1,0:T(8,128)(2,1)S(1)}, u32[]{:S(2)}, u32[]{:S(2)}) %all-to-all-start.2) | async-done | bytes 917536 | tf_op jit(solution)/shard_map/all_to_all | solution.py:69
  57.3 5.0 %all-to-all-start = ((bf16[32,16,896]{2,1,0:T(8,128)(2,1)}), bf16[32,16,896]{2,1,0:T(8,128)(2,1)}, u32[]{:S(2)}, u32[]{:S(2)}) async-start(bf16[32,16,896]{2,1,0:T(8,128)(2,1)} %bitcast.3), calls=%async_computation | async-start | bytes 1835008 | tf_op jit(solution)/shard_map/all_to_all | solution.py:68
  62.3 0.0 all-reduce.3.cloned.1.call-start
  62.4 0.0 copy-done
  62.4 2.3 fusion.17
  64.7 21.8 %all-to-all-done = bf16[32,16,896]{2,1,0:T(8,128)(2,1)} async-done(((bf16[32,16,896]{2,1,0:T(8,128)(2,1)}), bf16[32,16,896]{2,1,0:T(8,128)(2,1)}, u32[]{:S(2)}, u32[]{:S(2)}) %all-to-all-start) | async-done | bytes 917536 | tf_op jit(solution)/shard_map/all_to_all | solution.py:68
  86.4 6.0 %fusion.5 = bf16[512,2048]{1,0:T(8,128)(2,1)} fusion(bf16[512,896]{1,0:T(8,128)(2,1)} %bitcast.4, bf16[1,896,2048]{2,1,0:T(8,128)(2,1)} %param.10), kind=kOutput, calls=%fused_computation.8 | convolution fusion | flops 1880096768 | bytes 6684672 | tf_op jit(solution)/shard_map/dot_general | solution.py:73
  92.4 0.0 all-reduce.3.cloned.1.call-update
  92.4 160.4 %all-reduce.3.cloned.1.call-done = (bf16[512,2048]{1,0:T(8,128)(2,1)}, bf16[512,1024]{1,0:T(8,128)(2,1)}) async-done(((bf16[512,2048]{1,0:T(8,128)(2,1)}, bf16[512,1024]{1,0:T(8,128)(2,1)}), (bf16[512,2048]{1,0:T(8,128)(2,1)}, bf16[512,1024]{1,0:T(8,128)(2,1)})) %all-reduce.3.cloned.1.call-update) | async-done | bytes 3145744 | tf_op jit(solution)/shard_map/psum | solution.py:74
  252.9 2.2 convert_element_type.60
  255.1 0.0 copy-done.3
  255.1 0.0 copy-start.8
  255.1 2.3 fusion.10
  257.3 3.3 fusion.23
  260.6 10.7 %all-to-all-start.3 = ((bf16[32,16,896]{2,1,0:T(8,128)(2,1)}), bf16[32,16,896]{2,1,0:T(8,128)(2,1)}, u32[]{:S(2)}, u32[]{:S(2)}) async-start(bf16[32,16,896]{2,1,0:T(8,128)(2,1)} %bitcast.64), calls=%async_computation.3 | async-start | bytes 1835008 | tf_op jit(solution)/shard_map/all_to_all | solution.py:97
  271.3 3.4 %fusion.20 = bf16[512,896]{1,0:T(8,128)(2,1)} fusion(bf16[512,1024]{1,0:T(8,128)(2,1)} %get-tuple-element.8, bf16[1,1024,896]{2,1,0:T(8,128)(2,1)S(1)} %copy-done), kind=kOutput, calls=%fused_computation.26 | convolution fusion | flops 939982848 | bytes 3801088 | tf_op jit(solution)/shard_map/dot_general | solution.py:76
  274.7 20.7 %all-to-all-done.3 = bf16[32,16,896]{2,1,0:T(8,128)(2,1)} async-done(((bf16[32,16,896]{2,1,0:T(8,128)(2,1)}), bf16[32,16,896]{2,1,0:T(8,128)(2,1)}, u32[]{:S(2)}, u32[]{:S(2)}) %all-to-all-start.3) | async-done | bytes 917536 | tf_op jit(solution)/shard_map/all_to_all | solution.py:97
  295.4 5.0 %all-to-all-start.1 = ((bf16[32,16,896]{2,1,0:T(8,128)(2,1)}), bf16[32,16,896]{2,1,0:T(8,128)(2,1)}, u32[]{:S(2)}, u32[]{:S(2)}) async-start(bf16[32,16,896]{2,1,0:T(8,128)(2,1)} %bitcast.63), calls=%async_computation.1 | async-start | bytes 1835008 | tf_op jit(solution)/shard_map/all_to_all | solution.py:94
  300.4 4.1 %convert_bitcast_fusion.1 = bf16[1,1024,896]{2,1,0:T(8,128)(2,1)} fusion(bf16[512,1024]{1,0:T(8,128)(2,1)} %get-tuple-element.8, bf16[512,896]{1,0:T(8,128)(2,1)} %bitcast.62), kind=kOutput, calls=%fused_computation.23 | convolution fusion | flops 940441600 | bytes 3801088 | tf_op jit(solution)/shard_map/dot_general | solution.py:84
  304.5 5.1 %convert_bitcast_fusion = bf16[1,896,2048]{2,1,0:T(8,128)(2,1)} fusion(bf16[512,896]{1,0:T(8,128)(2,1)} %bitcast.4, bf16[512,1024]{1,0:T(8,128)(2,1)S(1)} %copy-done.2, bf16[512,1024]{1,0:T(8,128)(2,1)S(1)} %get-tuple-element.6), kind=kOutput, calls=%fused_computation.7 | convolution fusion | flops 1885077504 | bytes 6684672 | tf_op jit(solution)/shard_map/dot_general | solution.py:87
  309.6 2.4 convolution_convert_fusion.1
  312.1 12.5 %all-to-all-done.1 = bf16[32,16,896]{2,1,0:T(8,128)(2,1)} async-done(((bf16[32,16,896]{2,1,0:T(8,128)(2,1)}), bf16[32,16,896]{2,1,0:T(8,128)(2,1)}, u32[]{:S(2)}, u32[]{:S(2)}) %all-to-all-start.1) | async-done | bytes 917536 | tf_op jit(solution)/shard_map/all_to_all | solution.py:94
  324.5 3.1 convolution_convert_fusion.2
  (10 shorter events, 0.0 us)
Async XLA Ops:
  7.2 55.2 %copy-start = (bf16[1,1024,896]{2,1,0:T(8,128)(2,1)S(1)}, bf16[1,1024,896]{2,1,0:T(8,128)(2,1)}, u32[]{:S(2)}) copy-start(bf16[1,1024,896]{2,1,0:T(8,128)(2,1)} %param.11) | copy-start | bytes 5505028
  7.2 11.3 %copy-start.6 = (s32[256,8]{0,1:T(8,128)S(1)}, s32[256,8]{0,1:T(8,128)}, u32[]{:S(2)}) copy-start(s32[256,8]{0,1:T(8,128)} %param.8) | copy-start | bytes 24580
  7.2 13.3 %copy-start.7 = (f32[256,8]{0,1:T(8,128)S(1)}, f32[256,8]{0,1:T(8,128)}, u32[]{:S(2)}) copy-start(f32[256,8]{0,1:T(8,128)} %param.9) | copy-start | bytes 24580
  7.2 14.5 %copy-start.9 = (bf16[256,896]{1,0:T(8,128)(2,1)S(1)}, bf16[256,896]{1,0:T(8,128)(2,1)}, u32[]{:S(2)}) copy-start(bf16[256,896]{1,0:T(8,128)(2,1)} %param.7) | copy-start | bytes 1376260
  18.2 15.1 %copy-start.5 = (bf16[256,896]{1,0:T(8,128)(2,1)S(1)}, bf16[256,896]{1,0:T(8,128)(2,1)}, u32[]{:S(2)}) copy-start(bf16[256,896]{1,0:T(8,128)(2,1)} %param.6) | copy-start | bytes 1376260
  23.1 34.2 %all-to-all-start.2 = ((bf16[32,16,896]{2,1,0:T(8,128)(2,1)}), bf16[32,16,896]{2,1,0:T(8,128)(2,1)S(1)}, u32[]{:S(2)}, u32[]{:S(2)}) async-start(bf16[32,16,896]{2,1,0:T(8,128)(2,1)} %bitcast.65), calls=%async_computation.2 | async-start | bytes 1835008 | tf_op jit(solution)/shard_map/all_to_all | solution.py:69
  57.3 7.3 %copy-start.4 = (bf16[32,16,896]{2,1,0:T(8,128)(2,1)}, bf16[32,16,896]{2,1,0:T(8,128)(2,1)S(1)}, u32[]{:S(2)}) copy-start(bf16[32,16,896]{2,1,0:T(8,128)(2,1)S(1)} %all-to-all-done.2) | copy-start | bytes 2752516
  57.3 29.1 %all-to-all-start = ((bf16[32,16,896]{2,1,0:T(8,128)(2,1)}), bf16[32,16,896]{2,1,0:T(8,128)(2,1)}, u32[]{:S(2)}, u32[]{:S(2)}) async-start(bf16[32,16,896]{2,1,0:T(8,128)(2,1)} %bitcast.3), calls=%async_computation | async-start | bytes 1835008 | tf_op jit(solution)/shard_map/all_to_all | solution.py:68
  62.3 190.5 %all-reduce.3.cloned.1.call-start = ((), (), s32[]{:S(2)}) async-start(), calls=%async_computation.4 | async-start | bytes 6291456 | tf_op jit(solution)/shard_map/psum | solution.py:74
  252.9 2.2 copy-start.3
  255.1 2.3 copy-start.8
  257.3 3.3 copy-start.1
  260.6 34.8 %all-to-all-start.3 = ((bf16[32,16,896]{2,1,0:T(8,128)(2,1)}), bf16[32,16,896]{2,1,0:T(8,128)(2,1)}, u32[]{:S(2)}, u32[]{:S(2)}) async-start(bf16[32,16,896]{2,1,0:T(8,128)(2,1)} %bitcast.64), calls=%async_computation.3 | async-start | bytes 1835008 | tf_op jit(solution)/shard_map/all_to_all | solution.py:97
  295.4 29.1 %all-to-all-start.1 = ((bf16[32,16,896]{2,1,0:T(8,128)(2,1)}), bf16[32,16,896]{2,1,0:T(8,128)(2,1)}, u32[]{:S(2)}, u32[]{:S(2)}) async-start(bf16[32,16,896]{2,1,0:T(8,128)(2,1)} %bitcast.63), calls=%async_computation.1 | async-start | bytes 1835008 | tf_op jit(solution)/shard_map/all_to_all | solution.py:94
  300.4 4.1 %copy-start.2 = (bf16[512,1024]{1,0:T(8,128)(2,1)S(1)}, bf16[512,1024]{1,0:T(8,128)(2,1)}, u32[]{:S(2)}) copy-start(bf16[512,1024]{1,0:T(8,128)(2,1)} %copy-done.1) | copy-start | bytes 3145732
Sparse Core Ops, SparseCore 0:
  92.6 160.2 all-reduce.2
where the time goes:
time: 335 us; the launch traced here: 334 us
  waiting for transfers between devices  238 us (71%)
  matrix products  32.4 us (10%)
  starting transfers between devices  30.9 us (9%)
  other arithmetic  17.2 us (5%)
  between operations  14.2 us (4%)
    psum x1, waiting for transfers between devices, body(): lax.psum(partial_hidden.astype(jnp.bfloat16), 'dp').astype(jnp.float32)  160 us
    all_to_all x1, waiting for transfers between devices, body(): lax.all_to_all(cot_rows, 'expert', split_axis=0, concat_axis=0, tiled=True)  22.7 us
    all_to_all x1, waiting for transfers between devices, body(): lax.all_to_all(token_rows, 'expert', split_axis=0, concat_axis=0, tiled=T...  21.8 us
    all_to_all x1, waiting for transfers between devices, body(): lax.all_to_all(row_grad.reshape(send_shape), 'expert', split_axis=0, conc...  20.7 us
    all_to_all x1, waiting for transfers between devices, body(): lax.all_to_all(expert_out.reshape(send_shape), 'expert', split_axis=0, co...  12.5 us
    another operation x4, other arithmetic  11.7 us
    all_to_all x1, starting transfers between devices, body(): lax.all_to_all(row_grad.reshape(send_shape), 'expert', split_axis=0, conc...  10.7 us
    all_to_all x1, starting transfers between devices, body(): lax.all_to_all(cot_rows, 'expert', split_axis=0, concat_axis=0, tiled=True)  10.2 us
  transfers between devices with their start and end apart: 5, of which 5 were waited for; matrix products, arithmetic and copies ran while one was open for 6% of the time, Pallas kernels for 0%

commit v1 on v0

--- a/solution.py
+++ b/solution.py
@@ -71,7 +71,9 @@
     expert_rows = arrived[0].reshape(row_total, column_width)
     scaled_cot = arrived[1].reshape(row_total, column_width)
     partial_hidden = jnp.dot(expert_rows, inner_weight, preferred_element_type=jnp.float32)
-    hidden = lax.psum(partial_hidden.astype(jnp.bfloat16), "dp").astype(jnp.float32)
+    hidden = jnp.sum(lax.all_gather(partial_hidden.astype(jnp.bfloat16), "dp"), axis=0).astype(
+        jnp.float32
+    )
     active = activate(hidden, half_width)
     expert_out = jnp.dot(active, outer_weight, preferred_element_type=jnp.float32).astype(
         jnp.bfloat16

time: 335 us -> 566 us (1.69)
  waiting for transfers between devices: 238 us -> 361 us
  blocking collectives: 0 us -> 108 us
  other arithmetic: 17.2 us -> 32.5 us
  starting transfers between devices: 30.9 us -> 15.9 us
    all_gather x0 -> x1, waiting for transfers between devices: none -> 236 us  [body(): lax.all_gather(partial_hidden.astype(jnp.bfloat16), 'dp')]
    all_to_all x0 -> x2, blocking collectives: none -> 108 us  [the longest x1 73.7 us: body(): lax.all_to_all(cot_rows, 'expert', split_axis=0, concat_axis=0, tiled=True)]
    psum x1, waiting for transfers between devices: 160 us -> 90.8 us  [body(): lax.psum(partial_act.astype(jnp.bfloat16), 'dp').astype(jnp.float32)]
    all_to_all x2 -> x0, waiting for transfers between devices: 44.4 us -> none  [the longest x1 22.7 us: body(): lax.all_to_all(cot_rows, 'expert', split_axis=0, concat_axis=0, tiled=True)]
    all_to_all x2 -> x0, starting transfers between devices: 15.2 us -> none  [the longest x1 10.2 us: body(): lax.all_to_all(cot_rows, 'expert', split_axis=0, concat_axis=0, tiled=True)]
    reduce_sum x0 -> x1, other arithmetic: none -> 10.8 us  [body(): jnp.sum(lax.all_gather(partial_hidden.astype(jnp.bfloat16), 'dp'), axis=0)]
  transfers between devices with their start and end apart: 5 -> 4, of which waited for: 5 -> 4; matrix products, arithmetic and copies ran while one was open for 6% -> 6% of each run, Pallas kernels for 0% -> 0%
where the time goes in v1:
time: 566 us; the launch traced here: 565 us
  waiting for transfers between devices  361 us (64%)
  blocking collectives  108 us (19%)
  other arithmetic  32.5 us (6%)
  matrix products  29.2 us (5%)
  starting transfers between devices  15.9 us (3%)
  between operations  14.2 us (3%)
    all_gather x1, waiting for transfers between devices, body(): lax.all_gather(partial_hidden.astype(jnp.bfloat16), 'dp')  236 us
    psum x1, waiting for transfers between devices, body(): lax.psum(partial_act.astype(jnp.bfloat16), 'dp').astype(jnp.float32)  90.8 us
    all_to_all x1, blocking collectives, body(): lax.all_to_all(cot_rows, 'expert', split_axis=0, concat_axis=0, tiled=True)  73.7 us
    all_to_all x1, blocking collectives, body(): lax.all_to_all(token_rows, 'expert', split_axis=0, concat_axis=0, tiled=T...  34 us
    all_to_all x1, waiting for transfers between devices, body(): lax.all_to_all(row_grad.reshape(send_shape), 'expert', split_axis=0, conc...  20.7 us
    another operation x4, other arithmetic  14.4 us
    all_to_all x1, waiting for transfers between devices, body(): lax.all_to_all(expert_out.reshape(send_shape), 'expert', split_axis=0, co...  13.6 us
  transfers between devices with their start and end apart: 4, of which 4 were waited for; matrix products, arithmetic and copies ran while one was open for 6% of the time, Pallas kernels for 0%

profile of v1, /device:TPU:1, one launch (start us, length us, event | category | flops | bytes accessed | tf_op | source)
XLA Modules:
  0.0 565.0 jit_solution(16811683526052373065)
XLA Ops:
  7.2 0.0 copy-start
  7.2 0.0 copy-start.7
  7.2 0.0 copy-start.6
  7.2 0.0 all-gather.3.cloned.1.call-start
  7.2 1.0 copy.26
  8.2 0.1 eq.42
  8.3 0.1 eq.38
  8.5 9.1 %reduce-window.6 = s32[32,16,128]{2,1,0:T(8,128)S(1)} reduce-window(s32[32,16,128]{2,1,0:T(8,128)S(1)} %fusion.32, s32[]{:T(128)} %constant.5.clone.1), window={size=1x1x128 pad=0_0x0_0x127_0}, to_apply=%region_0.0 | reduce-window | flops 8323072 | bytes 524292 | tf_op jit(solution)/shard_map/reduce-window
  17.5 0.1 slice.18
  17.7 0.2 copy.31
  17.9 0.2 reduce-window.9
  18.1 0.1 broadcast_add_fusion
  18.3 0.1 fusion.29
  18.4 0.1 reduce_sum.33
  18.5 0.1 copy.30
  18.5 0.0 copy-done.7
  18.6 1.9 fusion
  20.5 0.0 copy-done.6
  20.5 0.4 convolution_convert_fusion
  20.9 34.0 %all_to_all.20 = bf16[32,16,896]{2,1,0:T(8,128)(2,1)S(1)} all-to-all(bf16[32,16,896]{2,1,0:T(8,128)(2,1)S(1)} %bitcast.62), channel_id=1, replica_groups=mesh['dp'=8,'expert'=32] {'expert'}, dimensions={0} | all-to-all | bytes 1835008 | tf_op jit(solution)/shard_map/all_to_all | solution.py:68
  55.0 1.0 copy-done.3
  55.9 5.7 %fusion.5 = bf16[512,2048]{1,0:T(8,128)(2,1)} fusion(bf16[512,896]{1,0:T(8,128)(2,1)S(1)} %bitcast.64, bf16[1,896,2048]{2,1,0:T(8,128)(2,1)} %param.10), kind=kOutput, calls=%fused_computation.8 | convolution fusion | flops 1880096768 | bytes 6684672 | tf_op jit(solution)/shard_map/dot_general | solution.py:73
  61.7 0.0 all-gather.3.cloned.1.call-update
  61.7 0.0 all-reduce.2.cloned.1.call-start
  61.7 0.6 copy-done.8
  62.4 1.3 select_reduce_fusion
  63.6 0.4 multiply_convert_fusion.1
  64.1 73.7 %all_to_all.21 = bf16[32,16,896]{2,1,0:T(8,128)(2,1)S(1)} all-to-all(bf16[32,16,896]{2,1,0:T(8,128)(2,1)S(1)} %bitcast.70), channel_id=1, replica_groups=mesh['dp'=8,'expert'=32] {'expert'}, dimensions={0} | all-to-all | bytes 1835008 | tf_op jit(solution)/shard_map/all_to_all | solution.py:69
  137.8 1.0 copy-done.5
  138.8 2.3 fusion.17
  141.0 0.0 all-reduce.2.cloned.1.call-update
  141.0 236.1 %all-gather.3.cloned.1.call-done = bf16[4096,2048]{1,0:T(8,128)(2,1)} async-done(((bf16[512,2048]{1,0:T(8,128)(2,1)}), bf16[4096,2048]{1,0:T(8,128)(2,1)}) %all-gather.3.cloned.1.call-update) | async-done | bytes 16777232 | tf_op jit(solution)/shard_map/all_gather | solution.py:74
  377.1 10.8 %reduce_sum.35 = bf16[512,2048]{1,0:T(8,128)(2,1)} reduce(bf16[8,512,2048]{2,1,0:T(8,128)(2,1)} %bitcast.61, bf16[]{:T(256)} %constant.16.clone.1), dimensions={0}, to_apply=%region_5.6 | reduce | flops 7340032 | bytes 18874370 | tf_op jit(solution)/shard_map/reduce_sum | solution.py:74
  387.9 4.0 convert_element_type.62
  391.9 90.8 %all-reduce.2.cloned.1.call-done = bf16[512,1024]{1,0:T(8,128)(2,1)} async-done(((bf16[512,1024]{1,0:T(8,128)(2,1)}), bf16[512,1024]{1,0:T(8,128)(2,1)}) %all-reduce.2.cloned.1.call-update) | async-done | bytes 1048592 | tf_op jit(solution)/shard_map/psum | solution.py:84
  482.8 4.9 fusion.10
  487.7 0.0 copy-done.9
  487.7 3.3 fusion.23
  491.0 10.8 %all-to-all-start.3 = ((bf16[32,16,896]{2,1,0:T(8,128)(2,1)}), bf16[32,16,896]{2,1,0:T(8,128)(2,1)}, u32[]{:S(2)}, u32[]{:S(2)}) async-start(bf16[32,16,896]{2,1,0:T(8,128)(2,1)} %bitcast.69), calls=%async_computation.3 | async-start | bytes 1835008 | tf_op jit(solution)/shard_map/all_to_all | solution.py:99
  501.9 3.4 fusion.20
  505.3 20.7 %all-to-all-done.3 = bf16[32,16,896]{2,1,0:T(8,128)(2,1)} async-done(((bf16[32,16,896]{2,1,0:T(8,128)(2,1)}), bf16[32,16,896]{2,1,0:T(8,128)(2,1)}, u32[]{:S(2)}, u32[]{:S(2)}) %all-to-all-start.3) | async-done | bytes 917536 | tf_op jit(solution)/shard_map/all_to_all | solution.py:99
  526.0 5.0 all-to-all-start.1
  531.0 4.2 convert_bitcast_fusion.1
  535.1 0.0 copy-done.4
  535.1 3.9 convert_bitcast_fusion
  539.1 2.4 convolution_convert_fusion.1
  541.5 13.6 %all-to-all-done.1 = bf16[32,16,896]{2,1,0:T(8,128)(2,1)} async-done(((bf16[32,16,896]{2,1,0:T(8,128)(2,1)}), bf16[32,16,896]{2,1,0:T(8,128)(2,1)}, u32[]{:S(2)}, u32[]{:S(2)}) %all-to-all-start.1) | async-done | bytes 917536 | tf_op jit(solution)/shard_map/all_to_all | solution.py:96
  555.1 3.1 convolution_convert_fusion.2
  (14 shorter events, 0.0 us)
Async XLA Ops:
  7.2 131.6 %copy-start = (bf16[1,1024,896]{2,1,0:T(8,128)(2,1)S(1)}, bf16[1,1024,896]{2,1,0:T(8,128)(2,1)}, u32[]{:S(2)}) copy-start(bf16[1,1024,896]{2,1,0:T(8,128)(2,1)} %param.11) | copy-start | bytes 5505028
  7.2 11.4 %copy-start.7 = (s32[256,8]{0,1:T(8,128)S(1)}, s32[256,8]{0,1:T(8,128)}, u32[]{:S(2)}) copy-start(s32[256,8]{0,1:T(8,128)} %param.8) | copy-start | bytes 24580
  7.2 13.3 %copy-start.6 = (bf16[256,896]{1,0:T(8,128)(2,1)S(1)}, bf16[256,896]{1,0:T(8,128)(2,1)}, u32[]{:S(2)}) copy-start(bf16[256,896]{1,0:T(8,128)(2,1)} %param.6) | copy-start | bytes 1376260
  7.2 369.9 %all-gather.3.cloned.1.call-start = ((), (), s32[]{:S(2)}) async-start(), calls=%async_computation.5 | async-start | bytes 18874368 | tf_op jit(solution)/shard_map/all_gather | solution.py:74
  55.0 1.0 copy-start.3
  61.7 0.7 copy-start.8
  61.7 2.0 copy-start.10
  61.7 421.1 %all-reduce.2.cloned.1.call-start = ((), (), s32[]{:S(2)}) async-start(), calls=%async_computation.4 | async-start | bytes 2097152 | tf_op jit(solution)/shard_map/psum | solution.py:84
  137.8 1.0 copy-start.5
  482.8 5.0 copy-start.9
  487.7 3.3 copy-start.1
  491.0 34.9 %all-to-all-start.3 = ((bf16[32,16,896]{2,1,0:T(8,128)(2,1)}), bf16[32,16,896]{2,1,0:T(8,128)(2,1)}, u32[]{:S(2)}, u32[]{:S(2)}) async-start(bf16[32,16,896]{2,1,0:T(8,128)(2,1)} %bitcast.69), calls=%async_computation.3 | async-start | bytes 1835008 | tf_op jit(solution)/shard_map/all_to_all | solution.py:99
  526.0 29.1 %all-to-all-start.1 = ((bf16[32,16,896]{2,1,0:T(8,128)(2,1)}), bf16[32,16,896]{2,1,0:T(8,128)(2,1)}, u32[]{:S(2)}, u32[]{:S(2)}) async-start(bf16[32,16,896]{2,1,0:T(8,128)(2,1)} %bitcast.68), calls=%async_computation.1 | async-start | bytes 1835008 | tf_op jit(solution)/shard_map/all_to_all | solution.py:96
  531.0 4.2 copy-start.2
  531.0 4.2 copy-start.4
Sparse Core Ops, SparseCore 0:
  61.8 315.2 all-gather.2
  380.3 102.4 all-reduce.1
